TPU v7x, 32 devices: a whole 2x2x4 slice. The times are simulated.
32 devices in a mesh: dp: 8 (over y, x, core), hid: 4 (over z).
Axes of the slice: x: 2, y: 2, z: 4, core: 2. Of those that a mesh axis runs over, the one named last changes fastest.
Arguments:
- tokens: bfloat16 [512, 4096], P(('dp', 'hid')), may hold values from -6 to 6
- cotangent: bfloat16 [512, 7680], P('dp', 'hid'), may hold values from -8 to 8
- weights: bfloat16 [2, 7680, 4096], P(None, 'hid'), may hold values from -0.09375 to 0.09375
- basis: bfloat16 [4096, 256], P('dp'), may hold values from -0.09375 to 0.09375
- master: float32 [2, 7680, 4096], P(None, 'hid', 'dp'), may hold values from -0.09375 to 0.09375
- first_moment: float32 [7680, 2, 256], P(('hid', 'dp')), may hold values from -48 to 48
- second_moment: float32 [7680, 2, 256], P(('hid', 'dp')), may hold values from 25 to 2500
Outputs:
- master_new: float32 [2, 7680, 4096], P(None, 'hid', 'dp')
- first_new: float32 [7680, 2, 256], P(('hid', 'dp'))
- second_new: float32 [7680, 2, 256], P(('hid', 'dp'))
All inputs are finite; a program needn't handle non-finite values.
Results may differ from a plain program's by a relative error of at most 0.0003.
Values may be sent and summed in bfloat16 or wider, within the bound.
No kernel may reach another device: no remote copies, remote signals or barrier semaphores. Data moves between devices by JAX's collectives and lax.ppermute only.
A program may use at most 128 MiB of HBM per device.

v0:
```python
import jax
import jax.numpy as jnp
from jax import lax
from jax.sharding import PartitionSpec as P

beta_first = 0.9
beta_second = 0.95
step_size = 0.05
adam_epsilon = 1e-08


def silu_pieces(pre_gate):
    sigmoid_val = jax.nn.sigmoid(pre_gate)
    return (pre_gate * sigmoid_val, sigmoid_val * (1.0 + pre_gate * (1.0 - sigmoid_val)))


def on_device(tokens, cotangent, weights, basis, master, first_moment, second_moment):
    highest = lax.Precision.HIGHEST
    group_tokens = lax.all_gather(tokens, "hid", axis=0, tiled=True)
    projected = jnp.dot(
        group_tokens,
        lax.all_gather(basis, "dp", axis=0, tiled=True),
        preferred_element_type=jnp.float32,
    )
    contract_cols = (((1,), (1,)), ((), ()))
    pre_gate = lax.dot_general(
        group_tokens, weights[0], contract_cols, preferred_element_type=jnp.float32
    )
    pre_up = lax.dot_general(
        group_tokens, weights[1], contract_cols, preferred_element_type=jnp.float32
    )
    activated, silu_slope = silu_pieces(pre_gate)
    upstream = cotangent.astype(jnp.float32)
    grad_gate = upstream * pre_up * silu_slope
    grad_up = upstream * activated
    over_tokens = (((0,), (0,)), ((), ()))
    gate_term = lax.dot_general(
        grad_gate, projected, over_tokens, precision=highest, preferred_element_type=jnp.float32
    )
    up_term = lax.dot_general(
        grad_up, projected, over_tokens, precision=highest, preferred_element_type=jnp.float32
    )
    gradient = lax.psum_scatter(
        jnp.stack([gate_term, up_term], axis=1), "dp", scatter_dimension=0, tiled=True
    )
    first_new = beta_first * first_moment + (1.0 - beta_first) * gradient
    second_new = beta_second * second_moment + (1.0 - beta_second) * gradient * gradient
    direction_share = first_new / (jnp.sqrt(second_new) + adam_epsilon)
    direction = lax.all_gather(direction_share, "dp", axis=0, tiled=True)
    lifted = jnp.einsum("fwr,dr->wfd", direction, basis.astype(jnp.float32), precision=highest)
    master_new = master - step_size * lifted
    return (master_new, first_new, second_new)


def solution(mesh):
    in_specs = (
        P(("dp", "hid"), None),
        P("dp", "hid"),
        P(None, "hid", None),
        P("dp", None),
        P(None, "hid", "dp"),
        P(("hid", "dp"), None, None),
        P(("hid", "dp"), None, None),
    )
    out_specs = (P(None, "hid", "dp"), P(("hid", "dp"), None, None), P(("hid", "dp"), None, None))
    return jax.shard_map(
        on_device, mesh=mesh, in_specs=in_specs, out_specs=out_specs, check_vma=False
    )
```

profile of v0, /device:TPU:0, one launch (start us, length us, event | category | flops | bytes accessed | tf_op | source)
XLA Modules:
  0.0 156.3 jit_solution(17608231928793287839)
XLA Ops:
  7.2 0.0 all-gather.3.cloned.1.call-start
  7.2 0.7 all-gather.3.cloned.1.call-update
  7.9 0.0 reduce-scatter.2.cloned.1.call-start
  7.9 17.6 %all_gather.9 = bf16[64,4096]{1,0:T(8,128)(2,1)S(1)} all-gather(bf16[16,4096]{1,0:T(8,128)(2,1)} %param.7), channel_id=1, replica_groups=mesh['dp'=8,'hid'=4] {'hid'}, dimensions={0}, use_global_device_ids=true | all-gather | bytes 655360 | tf_op jit(solution)/shard_map/all_gather | solution.py:19
  25.5 0.0 copy-start.3
  25.5 8.8 %fusion = f32[64,1920]{1,0:T(8,128)S(1)} fusion(bf16[64,4096]{1,0:T(8,128)(2,1)S(1)} %all_gather.9, bf16[2,1920,4096]{2,1,0:T(8,128)(2,1)} %param.9), kind=kOutput, calls=%fused_computation | convolution fusion | flops 1006632960 | bytes 16744448 | tf_op jit(solution)/shard_map/dot_general | solution.py:26
  34.3 0.0 copy-done.3
  34.3 8.8 %fusion.9 = f32[64,1920]{1,0:T(8,128)S(1)} fusion(bf16[64,4096]{1,0:T(8,128)(2,1)S(1)} %all_gather.9, bf16[2,1920,4096]{2,1,0:T(8,128)(2,1)} %param.9, bf16[64,1920]{1,0:T(8,128)(2,1)S(1)} %copy-done.3, f32[64,1920]{1,0:T(8,128)S(1)} %fusion), kind=kOutput, calls=%fused_computation.11 | convolution fusion | flops 1007861760 | bytes 17481728 | tf_op jit(solution)/shard_map/dot_general | solution.py:29
  43.2 0.0 all-gather.3.cloned.1.call-done
  43.2 2.0 %fusion.20 = f32[64,256]{1,0:T(8,128)S(1)} fusion(bf16[64,4096]{1,0:T(8,128)(2,1)S(1)} %all_gather.9, bf16[4096,256]{1,0:T(8,128)(2,1)} %all-gather.3.cloned.1.call-done), kind=kOutput, calls=%fused_computation.24 | convolution fusion | flops 134217728 | bytes 2686976 | tf_op jit(solution)/shard_map/dot_general | solution.py:20
  45.3 1.8 %convolution_bitcast_fusion = f32[1920,1,256]{2,0,1:T(8,128)S(1)} fusion(f32[64,256]{1,0:T(8,128)S(1)} %fusion.20, bf16[64,1920]{1,0:T(8,128)(2,1)S(1)} %copy-done.3, f32[64,1920]{1,0:T(8,128)S(1)} %fusion), kind=kOutput, calls=%fused_computation.8 | convolution fusion | flops 378224640 | bytes 2768896 | tf_op jit(solution)/shard_map/dot_general | solution.py:40
  47.0 1.8 %convolution_bitcast_fusion.1 = f32[1920,1,256]{2,0,1:T(8,128)S(1)} fusion(f32[64,1920]{1,0:T(8,128)S(1)} %fusion.9, f32[64,256]{1,0:T(8,128)S(1)} %fusion.20), kind=kOutput, calls=%fused_computation.9 | convolution fusion | flops 377487360 | bytes 2523136 | tf_op jit(solution)/shard_map/dot_general | solution.py:37
  48.8 2.2 %pad_maximum_fusion = f32[1920,2,256]{2,0,1:T(8,128)} fusion(f32[1920,1,256]{2,0,1:T(8,128)S(1)} %convolution_bitcast_fusion, f32[1920,1,256]{2,0,1:T(8,128)S(1)} %convolution_bitcast_fusion.1), kind=kLoop, calls=%fused_computation.7 | loop fusion | flops 983040 | bytes 7864320 | tf_op jit(solution)/shard_map/stack | solution.py:44
  51.0 0.0 copy-start.1
  51.0 0.0 copy-start.2
  51.0 0.0 copy-start
  51.0 0.0 reduce-scatter.2.cloned.1.call-update
  51.0 0.0 all-gather.5.cloned.1.call-start
  51.1 51.6 %reduce-scatter.2.cloned.1.call-done = f32[240,2,256]{2,0,1:T(8,128)} async-done(((f32[1920,2,256]{2,0,1:T(8,128)}), f32[240,2,256]{2,0,1:T(8,128)}) %reduce-scatter.2.cloned.1.call-update) | async-done | bytes 491536 | tf_op jit(solution)/shard_map/reduce_scatter | solution.py:43
  102.7 0.0 copy-done.1
  102.7 0.0 copy-done.2
  102.7 2.1 %add_divide_fusion = (f32[240,2,256]{2,0,1:T(8,128)}, f32[240,2,256]{2,0,1:T(8,128)S(1)}, f32[240,2,256]{2,0,1:T(8,128)S(1)}) fusion(f32[240,2,256]{2,0,1:T(8,128)} %reduce-scatter.2.cloned.1.call-done, f32[240,2,256]{2,1,0:T(2,128)S(1)} %copy-done.1, f32[240,2,256]{2,1,0:T(2,128)S(1)} %copy-done.2), kind=kLoop, calls=%fused_computation.18 | loop fusion | flops 1105920 | bytes 2949120 | tf_op jit(solution)/shard_map/div | solution.py:48
  104.8 0.0 all-gather.5.cloned.1.call-update
  104.8 1.2 copy.13
  106.0 1.2 copy.12
  107.1 33.5 %all-gather.5.cloned.1.call-done = f32[1920,2,256]{2,0,1:T(8,128)} async-done(((f32[240,2,256]{2,0,1:T(8,128)}), f32[1920,2,256]{2,0,1:T(8,128)}) %all-gather.5.cloned.1.call-update) | async-done | bytes 3932176 | tf_op jit(solution)/shard_map/all_gather | solution.py:49
  140.7 0.0 copy-done
  140.7 9.1 %bitcast_subtract_fusion = f32[2,1920,512]{2,1,0:T(8,128)} fusion(f32[2,1920,512]{2,1,0:T(8,128)} %param.11, f32[1920,2,256]{2,0,1:T(8,128)} %all-gather.5.cloned.1.call-done, bf16[512,256]{1,0:T(8,128)(2,1)S(1)} %copy-done), kind=kOutput, calls=%fused_computation.6 | convolution fusion | flops 6043729920 | bytes 19922944 | tf_op jit(solution)/shard_map/fwr,dr->wfd/dot_general | solution.py:50
Async XLA Ops:
  7.2 36.0 %all-gather.3.cloned.1.call-start = ((), (), s32[]{:S(2)}) async-start(), calls=%async_computation.1 | async-start | bytes 2359296 | tf_op jit(solution)/shard_map/all_gather | solution.py:22
  7.9 94.8 %reduce-scatter.2.cloned.1.call-start = ((), (), s32[]{:S(2)}) async-start(), calls=%async_computation.2 | async-start | bytes 4423680 | tf_op jit(solution)/shard_map/reduce_scatter | solution.py:43
  25.5 8.8 %copy-start.3 = (bf16[64,1920]{1,0:T(8,128)(2,1)S(1)}, bf16[64,1920]{1,0:T(8,128)(2,1)}, u32[]{:S(2)}) copy-start(bf16[64,1920]{1,0:T(8,128)(2,1)} %param.8) | copy-start | bytes 737284
  51.0 51.7 %copy-start.1 = (f32[240,2,256]{2,1,0:T(2,128)S(1)}, f32[240,2,256]{2,1,0:T(2,128)}, u32[]{:S(2)}) copy-start(f32[240,2,256]{2,1,0:T(2,128)} %param.13) | copy-start | bytes 1474564
  51.0 51.7 %copy-start.2 = (f32[240,2,256]{2,1,0:T(2,128)S(1)}, f32[240,2,256]{2,1,0:T(2,128)}, u32[]{:S(2)}) copy-start(f32[240,2,256]{2,1,0:T(2,128)} %param.12) | copy-start | bytes 1474564
  51.0 89.7 %copy-start = (bf16[512,256]{1,0:T(8,128)(2,1)S(1)}, bf16[512,256]{1,0:T(8,128)(2,1)}, u32[]{:S(2)}) copy-start(bf16[512,256]{1,0:T(8,128)(2,1)} %param.10) | copy-start | bytes 786436
  51.0 89.7 %all-gather.5.cloned.1.call-start = ((), (), s32[]{:S(2)}) async-start(), calls=%async_computation.3 | async-start | bytes 4423680 | tf_op jit(solution)/shard_map/all_gather | solution.py:49
Sparse Core Ops, SparseCore 0:
  9.9 30.4 all-gather.2
  51.1 51.5 reduce-scatter.1
  105.2 35.4 all-gather.4
where the time goes:
time: 156 us
  waiting for transfers between devices  85.9 us (55%)
  matrix products  32.3 us (21%)
  blocking collectives  17.6 us (11%)
  between operations  13.8 us (9%)
  other arithmetic  4.27 us (3%)
  local copies, waits for them, and re-layouts  2.33 us (1%)
    reduce_scatter x1, waiting for transfers between devices, on_device(): lax.psum_scatter(jnp.stack([gate_term, up_term], axis=1), 'dp', scatter_d...  51.6 us
    all_gather x1, waiting for transfers between devices, on_device(): direction = lax.all_gather(direction_share, 'dp', axis=0, tiled=True)  33.5 us
    all_gather x1, blocking collectives, on_device(): group_tokens = lax.all_gather(tokens, 'hid', axis=0, tiled=True)  17.6 us
    dot_general x1, matrix products, on_device(): jnp.einsum('fwr,dr->wfd', direction, basis.astype(jnp.float32), precision...  9.06 us
    dot_general x1, matrix products, on_device(): lax.dot_general(group_tokens, weights[1], contract_cols, preferred_elemen...  8.84 us
    dot_general x1, matrix products, on_device(): lax.dot_general(group_tokens, weights[0], contract_cols, preferred_elemen...  8.77 us
  transfers between devices with their start and end apart: 3, of which 2 were waited for; matrix products, arithmetic and copies ran while one was open for 13% of the time, Pallas kernels for 0%

commit v1 on v0

--- a/solution.py
+++ b/solution.py
@@ -46,7 +46,12 @@
     first_new = beta_first * first_moment + (1.0 - beta_first) * gradient
     second_new = beta_second * second_moment + (1.0 - beta_second) * gradient * gradient
     direction_share = first_new / (jnp.sqrt(second_new) + adam_epsilon)
-    direction = lax.all_gather(direction_share, "dp", axis=0, tiled=True)
+    ring = [direction_share]
+    for hop in range(7):
+        ring.append(lax.ppermute(ring[-1], "dp", [(dev, (dev + 1) % 8) for dev in range(8)]))
+    direction = jnp.roll(
+        jnp.concatenate(ring[::-1], axis=0), (lax.axis_index("dp") + 1) * ring[0].shape[0], axis=0
+    )
     lifted = jnp.einsum("fwr,dr->wfd", direction, basis.astype(jnp.float32), precision=highest)
     master_new = master - step_size * lifted
     return (master_new, first_new, second_new)

time: 156 us -> 189 us (1.21)
  waiting for transfers between devices: 85.9 us -> 115 us
  local copies, waits for them, and re-layouts: 2.33 us -> 9 us
  matrix products: 32.3 us -> 29.3 us
    ppermute x0 -> x7, waiting for transfers between devices: none -> 62.1 us  [on_device(): lax.ppermute(ring[-1], 'dp', [(dev, (dev + 1) % 8) for dev in range(8)])]
    all_gather x1 -> x0, waiting for transfers between devices: 33.5 us -> none  [on_device(): direction = lax.all_gather(direction_share, 'dp', axis=0, tiled=True)]
    unnamed x10 -> x33, local copies, waits for them, and re-layouts: 2.33 us -> 8.97 us
    dot_general x1, matrix products: 9.06 us -> 6.1 us  [on_device(): jnp.einsum('fwr,dr->wfd', direction, basis.astype(jnp.float32), precision...]
  transfers between devices with their start and end apart: 3 -> 9, of which waited for: 2 -> 8; matrix products, arithmetic and copies ran while one was open for 13% -> 11% of each run, Pallas kernels for 0% -> 0%
where the time goes in v1:
time: 189 us; the launch traced here: 188 us
  waiting for transfers between devices  115 us (61%)
  matrix products  29.3 us (16%)
  blocking collectives  17.6 us (9%)
  between operations  14.3 us (8%)
  local copies, waits for them, and re-layouts  9 us (5%)
  other arithmetic  3.49 us (2%)
    ppermute x7, waiting for transfers between devices, on_device(): lax.ppermute(ring[-1], 'dp', [(dev, (dev + 1) % 8) for dev in range(8)])  62.1 us
    reduce_scatter x1, waiting for transfers between devices, on_device(): lax.psum_scatter(jnp.stack([gate_term, up_term], axis=1), 'dp', scatter_d...  51.7 us
    all_gather x1, blocking collectives, on_device(): group_tokens = lax.all_gather(tokens, 'hid', axis=0, tiled=True)  17.6 us
    unnamed x33, local copies, waits for them, and re-layouts  8.97 us
    dot_general x1, matrix products, on_device(): lax.dot_general(group_tokens, weights[1], contract_cols, preferred_elemen...  8.84 us
    dot_general x1, matrix products, on_device(): lax.dot_general(group_tokens, weights[0], contract_cols, preferred_elemen...  8.77 us
    dot_general x1, matrix products, on_device(): jnp.einsum('fwr,dr->wfd', direction, basis.astype(jnp.float32), precision...  6.1 us
  transfers between devices with their start and end apart: 9, of which 8 were waited for; matrix products, arithmetic and copies ran while one was open for 11% of the time, Pallas kernels for 0%

profile of v1, /device:TPU:0, one launch (start us, length us, event | category | flops | bytes accessed | tf_op | source)
XLA Modules:
  0.0 188.4 jit_solution(8967825339956676141)
XLA Ops:
  7.2 0.0 all-gather.2.cloned.1.call-start
  7.2 0.7 all-gather.2.cloned.1.call-update
  7.9 0.0 reduce-scatter.2.cloned.1.call-start
  7.9 17.6 %all_gather.6 = bf16[64,4096]{1,0:T(8,128)(2,1)S(1)} all-gather(bf16[16,4096]{1,0:T(8,128)(2,1)} %param.7), channel_id=1, replica_groups=mesh['dp'=8,'hid'=4] {'hid'}, dimensions={0}, use_global_device_ids=true | all-gather | bytes 655360 | tf_op jit(solution)/shard_map/all_gather | solution.py:19
  25.5 0.0 copy-start.5
  25.5 8.8 %fusion = f32[64,1920]{1,0:T(8,128)S(1)} fusion(bf16[64,4096]{1,0:T(8,128)(2,1)S(1)} %all_gather.6, bf16[2,1920,4096]{2,1,0:T(8,128)(2,1)} %param.9), kind=kOutput, calls=%fused_computation | convolution fusion | flops 1006632960 | bytes 16744448 | tf_op jit(solution)/shard_map/dot_general | solution.py:26
  34.3 0.0 copy-done.5
  34.3 8.8 %fusion.10 = f32[64,1920]{1,0:T(8,128)S(1)} fusion(bf16[64,4096]{1,0:T(8,128)(2,1)S(1)} %all_gather.6, bf16[2,1920,4096]{2,1,0:T(8,128)(2,1)} %param.9, bf16[64,1920]{1,0:T(8,128)(2,1)S(1)} %copy-done.5, f32[64,1920]{1,0:T(8,128)S(1)} %fusion), kind=kOutput, calls=%fused_computation.12 | convolution fusion | flops 1007861760 | bytes 17481728 | tf_op jit(solution)/shard_map/dot_general | solution.py:29
  43.2 0.0 all-gather.2.cloned.1.call-done
  43.2 2.0 %fusion.22 = f32[64,256]{1,0:T(8,128)S(1)} fusion(bf16[64,4096]{1,0:T(8,128)(2,1)S(1)} %all_gather.6, bf16[4096,256]{1,0:T(8,128)(2,1)} %all-gather.2.cloned.1.call-done), kind=kOutput, calls=%fused_computation.42 | convolution fusion | flops 134217728 | bytes 2686976 | tf_op jit(solution)/shard_map/dot_general | solution.py:20
  45.3 0.0 copy-start.3
  45.3 0.0 copy-start.4
  45.3 1.8 convolution_bitcast_fusion
  47.1 1.8 convolution_bitcast_fusion.1
  48.8 2.2 %pad_maximum_fusion = f32[1920,2,256]{2,0,1:T(8,128)} fusion(f32[1920,1,256]{2,0,1:T(8,128)S(1)} %convolution_bitcast_fusion, f32[1920,1,256]{2,0,1:T(8,128)S(1)} %convolution_bitcast_fusion.1), kind=kLoop, calls=%fused_computation.7 | loop fusion | flops 983040 | bytes 7864320 | tf_op jit(solution)/shard_map/stack | solution.py:44
  51.0 0.0 reduce-scatter.2.cloned.1.call-update
  51.0 51.7 %reduce-scatter.2.cloned.1.call-done = f32[240,2,256]{2,0,1:T(8,128)} async-done(((f32[1920,2,256]{2,0,1:T(8,128)}), f32[240,2,256]{2,0,1:T(8,128)}) %reduce-scatter.2.cloned.1.call-update) | async-done | bytes 491536 | tf_op jit(solution)/shard_map/reduce_scatter | solution.py:43
  102.7 0.0 copy-done.3
  102.7 0.0 copy-done.4
  102.7 1.3 add_divide_fusion
  104.0 0.1 collective-permute-start
  104.1 9.1 %collective-permute-done = f32[240,2,256]{2,0,1:T(8,128)S(1)} collective-permute-done((f32[240,2,256]{2,0,1:T(8,128)S(1)}, f32[240,2,256]{2,0,1:T(8,128)S(1)}, u32[]{:S(2)}, u32[]{:S(2)}) %collective-permute-start) | collective-permute-done | bytes 491552 | tf_op jit(solution)/shard_map/ppermute | solution.py:51
  113.2 0.0 collective-permute-start.1
  113.2 9.2 %collective-permute-done.1 = f32[240,2,256]{2,0,1:T(8,128)S(1)} collective-permute-done((f32[240,2,256]{2,0,1:T(8,128)S(1)}, f32[240,2,256]{2,0,1:T(8,128)S(1)}, u32[]{:S(2)}, u32[]{:S(2)}) %collective-permute-start.1) | collective-permute-done | bytes 491552 | tf_op jit(solution)/shard_map/ppermute | solution.py:51
  122.4 0.0 collective-permute-start.2
  122.4 9.2 %collective-permute-done.2 = f32[240,2,256]{2,0,1:T(8,128)S(1)} collective-permute-done((f32[240,2,256]{2,0,1:T(8,128)S(1)}, f32[240,2,256]{2,0,1:T(8,128)S(1)}, u32[]{:S(2)}, u32[]{:S(2)}) %collective-permute-start.2) | collective-permute-done | bytes 491552 | tf_op jit(solution)/shard_map/ppermute | solution.py:51
  131.6 0.0 collective-permute-start.3
  131.6 9.2 %collective-permute-done.3 = f32[240,2,256]{2,0,1:T(8,128)S(1)} collective-permute-done((f32[240,2,256]{2,0,1:T(8,128)S(1)}, f32[240,2,256]{2,0,1:T(8,128)S(1)}, u32[]{:S(2)}, u32[]{:S(2)}) %collective-permute-start.3) | collective-permute-done | bytes 491552 | tf_op jit(solution)/shard_map/ppermute | solution.py:51
  140.7 0.0 collective-permute-start.4
  140.7 9.2 %collective-permute-done.4 = f32[240,2,256]{2,0,1:T(8,128)S(1)} collective-permute-done((f32[240,2,256]{2,0,1:T(8,128)S(1)}, f32[240,2,256]{2,0,1:T(8,128)S(1)}, u32[]{:S(2)}, u32[]{:S(2)}) %collective-permute-start.4) | collective-permute-done | bytes 491552 | tf_op jit(solution)/shard_map/ppermute | solution.py:51
  149.9 0.0 copy-start
  149.9 0.8 copy-done
  150.6 0.0 collective-permute-start.5
  150.6 9.3 %collective-permute-done.5 = f32[240,2,256]{2,0,1:T(8,128)} collective-permute-done((f32[240,2,256]{2,0,1:T(8,128)S(1)}, f32[240,2,256]{2,0,1:T(8,128)}, u32[]{:S(2)}, u32[]{:S(2)}) %collective-permute-start.5) | collective-permute-done | bytes 491552 | tf_op jit(solution)/shard_map/ppermute | solution.py:51
  159.9 0.0 collective-permute-start.6
  159.9 0.0 copy-start.1
  159.9 1.2 copy.12
  161.1 1.2 copy.13
  162.2 0.0 slice-start
  162.2 0.0 copy-start.2
  162.2 7.1 %collective-permute-done.6 = f32[240,2,256]{2,0,1:T(8,128)} collective-permute-done((f32[240,2,256]{2,0,1:T(8,128)}, f32[240,2,256]{2,0,1:T(8,128)}, u32[]{:S(2)}, u32[]{:S(2)}) %collective-permute-start.6) | collective-permute-done | bytes 491552 | tf_op jit(solution)/shard_map/ppermute | solution.py:51
  169.4 1.1 constant_dynamic-update-slice_fusion.15
  170.4 1.1 constant_dynamic-update-slice_fusion.14
  171.5 1.1 constant_dynamic-update-slice_fusion.13
  172.8 0.0 slice-start.1
  172.8 1.2 constant_dynamic-update-slice_fusion.7
  174.0 1.1 constant_dynamic-update-slice_fusion.6
  175.1 0.0 copy-done.1
  175.4 0.0 slice-done
  175.4 0.0 copy-done.2
  175.4 0.0 slice-done.1
  175.4 6.1 %bitcast_subtract_fusion = f32[2,1920,512]{2,1,0:T(8,128)} fusion(f32[2,1920,512]{2,1,0:T(8,128)S(1)} %bitcast.27, f32[3840,2,256]{2,0,1:T(8,128)S(1)} %constant_dynamic-update-slice_fusion, s32[]{:T(128)S(6)} %select_n.14, bf16[512,256]{1,0:T(8,128)(2,1)S(1)} %copy-done.2), kind=kOutput, calls=%fused_computation.6 | convolution fusion | flops 6043729920 | bytes 19922948 | tf_op jit(solution)/shard_map/fwr,dr->wfd/dot_general | solution.py:55
  (12 shorter events, 0.4 us)
Async XLA Ops:
  7.2 36.0 %all-gather.2.cloned.1.call-start = ((), (), s32[]{:S(2)}) async-start(), calls=%async_computation.1 | async-start | bytes 2359296 | tf_op jit(solution)/shard_map/all_gather | solution.py:22
  7.9 94.8 %reduce-scatter.2.cloned.1.call-start = ((), (), s32[]{:S(2)}) async-start(), calls=%async_computation.2 | async-start | bytes 4423680 | tf_op jit(solution)/shard_map/reduce_scatter | solution.py:43
  25.5 8.8 %copy-start.5 = (bf16[64,1920]{1,0:T(8,128)(2,1)S(1)}, bf16[64,1920]{1,0:T(8,128)(2,1)}, u32[]{:S(2)}) copy-start(bf16[64,1920]{1,0:T(8,128)(2,1)} %param.8) | copy-start | bytes 737284
  45.3 57.5 %copy-start.3 = (f32[240,2,256]{2,1,0:T(2,128)S(1)}, f32[240,2,256]{2,1,0:T(2,128)}, u32[]{:S(2)}) copy-start(f32[240,2,256]{2,1,0:T(2,128)} %param.13) | copy-start | bytes 1474564
  45.3 57.5 %copy-start.4 = (f32[240,2,256]{2,1,0:T(2,128)S(1)}, f32[240,2,256]{2,1,0:T(2,128)}, u32[]{:S(2)}) copy-start(f32[240,2,256]{2,1,0:T(2,128)} %param.12) | copy-start | bytes 1474564
  104.0 9.2 %collective-permute-start = (f32[240,2,256]{2,0,1:T(8,128)S(1)}, f32[240,2,256]{2,0,1:T(8,128)S(1)}, u32[]{:S(2)}, u32[]{:S(2)}) collective-permute-start(f32[240,2,256]{2,0,1:T(8,128)S(1)} %get-tuple-element.6), channel_id=1, source_target_pairs={{0,4},{4,8},{8,12},{12,16},{16,20},{20,24},{24,28},{28,0},{1,5},{5... | collective-permute-start | bytes 1474568 | tf_op jit(solution)/shard_map/ppermute | solution.py:51
  113.2 9.2 %collective-permute-start.1 = (f32[240,2,256]{2,0,1:T(8,128)S(1)}, f32[240,2,256]{2,0,1:T(8,128)S(1)}, u32[]{:S(2)}, u32[]{:S(2)}) collective-permute-start(f32[240,2,256]{2,0,1:T(8,128)S(1)} %collective-permute-done), channel_id=1, source_target_pairs={{0,4},{4,8},{8,12},{12,16},{16,20},{20,24},{24,28},{28,0},{1,5},{5... | collective-permute-start | bytes 1474568 | tf_op jit(solution)/shard_map/ppermute | solution.py:51
  122.4 9.2 %collective-permute-start.2 = (f32[240,2,256]{2,0,1:T(8,128)S(1)}, f32[240,2,256]{2,0,1:T(8,128)S(1)}, u32[]{:S(2)}, u32[]{:S(2)}) collective-permute-start(f32[240,2,256]{2,0,1:T(8,128)S(1)} %collective-permute-done.1), channel_id=1, source_target_pairs={{0,4},{4,8},{8,12},{12,16},{16,20},{20,24},{24,28},{28,0},{1,5},{5... | collective-permute-start | bytes 1474568 | tf_op jit(solution)/shard_map/ppermute | solution.py:51
  131.6 9.2 %collective-permute-start.3 = (f32[240,2,256]{2,0,1:T(8,128)S(1)}, f32[240,2,256]{2,0,1:T(8,128)S(1)}, u32[]{:S(2)}, u32[]{:S(2)}) collective-permute-start(f32[240,2,256]{2,0,1:T(8,128)S(1)} %collective-permute-done.2), channel_id=1, source_target_pairs={{0,4},{4,8},{8,12},{12,16},{16,20},{20,24},{24,28},{28,0},{1,5},{5... | collective-permute-start | bytes 1474568 | tf_op jit(solution)/shard_map/ppermute | solution.py:51
  140.7 9.2 %collective-permute-start.4 = (f32[240,2,256]{2,0,1:T(8,128)S(1)}, f32[240,2,256]{2,0,1:T(8,128)S(1)}, u32[]{:S(2)}, u32[]{:S(2)}) collective-permute-start(f32[240,2,256]{2,0,1:T(8,128)S(1)} %collective-permute-done.3), channel_id=1, source_target_pairs={{0,4},{4,8},{8,12},{12,16},{16,20},{20,24},{24,28},{28,0},{1,5},{5... | collective-permute-start | bytes 1474568 | tf_op jit(solution)/shard_map/ppermute | solution.py:51
  149.9 0.8 copy-start
  150.6 9.3 %collective-permute-start.5 = (f32[240,2,256]{2,0,1:T(8,128)S(1)}, f32[240,2,256]{2,0,1:T(8,128)}, u32[]{:S(2)}, u32[]{:S(2)}) collective-permute-start(f32[240,2,256]{2,0,1:T(8,128)S(1)} %collective-permute-done.4), channel_id=1, source_target_pairs={{0,4},{4,8},{8,12},{12,16},{16,20},{20,24},{24,28},{28,0},{1,5},{5... | collective-permute-start | bytes 1474568 | tf_op jit(solution)/shard_map/ppermute | solution.py:51
  159.9 9.5 %collective-permute-start.6 = (f32[240,2,256]{2,0,1:T(8,128)}, f32[240,2,256]{2,0,1:T(8,128)}, u32[]{:S(2)}, u32[]{:S(2)}) collective-permute-start(f32[240,2,256]{2,0,1:T(8,128)} %collective-permute-done.5), channel_id=1, source_target_pairs={{0,4},{4,8},{8,12},{12,16},{16,20},{20,24},{24,28},{28,0},{1,5},{5... | collective-permute-start | bytes 1474568 | tf_op jit(solution)/shard_map/ppermute | solution.py:51
  159.9 15.2 %copy-start.1 = (f32[240,2,256]{2,0,1:T(8,128)S(1)}, f32[240,2,256]{2,0,1:T(8,128)}, u32[]{:S(2)}) copy-start(f32[240,2,256]{2,0,1:T(8,128)} %copy-done) | copy-start | bytes 1474564
  162.2 13.2 %slice-start = ((s8[7864320]{0:T(1024)(128)(4,1)}), s8[4194304]{0:T(1024)(128)(4,1)S(1)}, s32[]{:S(2)}) async-start(s8[7864320]{0:T(1024)(128)(4,1)} %bitcast.26), calls=%async_computation.3 | async-start | bytes 8388608
  162.2 13.2 %copy-start.2 = (bf16[512,256]{1,0:T(8,128)(2,1)S(1)}, bf16[512,256]{1,0:T(8,128)(2,1)}, u32[]{:S(2)}) copy-start(bf16[512,256]{1,0:T(8,128)(2,1)} %param.10) | copy-start | bytes 786436
  172.8 2.6 %slice-start.1 = ((s8[7864320]{0:T(1024)(128)(4,1)}), s8[3670016]{0:T(1024)(128)(4,1)S(1)}, s32[]{:S(2)}) async-start(s8[7864320]{0:T(1024)(128)(4,1)} %bitcast.26), calls=%async_computation.4 | async-start | bytes 7340032
Sparse Core Ops, SparseCore 0:
  9.9 30.4 all-gather.1
  51.1 51.5 reduce-scatter.1
